TPU v7x, 512 devices: a whole 4x8x8 slice. The times are simulated.
512 devices in a mesh: grp: 16 (over x, z_lo, core), blk: 32 (over z_hi, y).
Axes of the slice: x: 4, y: 8, z: 8 (z_hi: 4, z_lo: 2; z = z_hi * 2 + z_lo), core: 2. Of those that a mesh axis runs over, the one named last changes fastest.
Arguments:
- particles: bfloat16 [1024, 2, 4000], P(('blk', 'grp')), may hold values from -6 to 6
- ctf_class: int32 [1024], P(('blk', 'grp')), may hold values from 0 to 63
- orient_prior: bfloat16 [1024, 192], P(('blk', 'grp')), may hold values from -6 to 6
- ctf_curves: float32 [64, 4000], replicated, may hold values from -1 to 1
- noise_weight: float32 [4000], replicated, may hold values from 0.005 to 0.05
- shift_phase: float32 [9, 4000], replicated, may hold values from -3.140625 to 3.140625
- trans_index: int32 [9], replicated, may hold values from 0 to 8, each once
- projections: bfloat16 [4096, 2, 4000], P(('grp', 'blk')), may hold values from -1.75 to 1.75
- orient_subset: int32 [4096], P(('grp', 'blk')), may hold values from 0 to 191
Outputs:
- scores: float32 [1024, 9, 4096], P('blk', None, 'grp')
Inputs may be any that keep to these rules, and one draw needn't show every extreme that they name: `trans_index`: each row of shift_phase is named once.
All inputs are finite; a program needn't handle non-finite values.
Results may differ from a plain program's by a relative error of at most 0.00056.
Values may be sent and summed in bfloat16 or wider, within the bound.
A program may use at most 128 MiB of HBM per device.

v0:
```python
import jax
import jax.numpy as jnp
from jax import lax
from jax.sharding import PartitionSpec as P


def per_device(
    particles,
    ctf_class,
    orient_prior,
    ctf_curves,
    noise_weight,
    shift_phase,
    trans_index,
    projections,
    orient_subset,
):
    highest = lax.Precision.HIGHEST
    classes_count = ctf_curves.shape[0]
    subset_count = orient_prior.shape[1]
    shift_count = shift_phase.shape[0]
    weight_rows = ctf_curves * noise_weight[None, :]

    def class_onehot(classes):
        return (classes[:, None] == jnp.arange(classes_count, dtype=jnp.int32)[None, :]).astype(
            jnp.float32
        )

    curve_local = jnp.dot(class_onehot(ctf_class), weight_rows, precision=highest)
    local_weighted = (particles.astype(jnp.float32) * curve_local[:, None, :]).astype(jnp.bfloat16)
    weighted, classes, prior = (
        lax.all_gather(local_weighted, "grp", axis=0, tiled=True),
        lax.all_gather(ctf_class, "grp", axis=0, tiled=True),
        lax.all_gather(orient_prior, "grp", axis=0, tiled=True),
    )
    onehot_rows = class_onehot(classes)
    prior_wide = prior.astype(jnp.float32)
    pick_shift = (trans_index[:, None] == jnp.arange(shift_count, dtype=jnp.int32)[None, :]).astype(
        jnp.float32
    )
    angle = jnp.dot(pick_shift, shift_phase, precision=highest)
    cos_part = jnp.cos(angle)
    sin_part = jnp.sin(angle)
    curve_sq = ctf_curves * ctf_curves * noise_weight[None, :]
    bank = lax.all_gather(projections, "blk", axis=0, tiled=True)
    subset_ids = lax.all_gather(orient_subset, "blk", axis=0, tiled=True)
    bank_real = bank[:, 0, :].astype(jnp.float32)
    bank_imag = bank[:, 1, :].astype(jnp.float32)
    real_shift = cos_part[:, None, :] * bank_real[None] + sin_part[:, None, :] * bank_imag[None]
    imag_shift = cos_part[:, None, :] * bank_imag[None] - sin_part[:, None, :] * bank_real[None]
    shifted = jnp.stack([real_shift, imag_shift], axis=2).astype(jnp.bfloat16)
    cross = jnp.einsum("nck,tmck->ntm", weighted, shifted, preferred_element_type=jnp.float32)
    power = bank_real * bank_real + bank_imag * bank_imag
    norm_table = jnp.dot(curve_sq, power.T, precision=highest)
    norm_sel = jnp.dot(onehot_rows, norm_table, precision=highest)
    subset_onehot = (
        subset_ids[None, :] == jnp.arange(subset_count, dtype=jnp.int32)[:, None]
    ).astype(jnp.float32)
    prior_term = jnp.dot(prior_wide, subset_onehot, precision=highest)
    return cross - 0.5 * norm_sel[:, None, :] + prior_term[:, None, :]


def solution(mesh):
    placed = (
        P(("blk", "grp"), None, None),
        P(("blk", "grp")),
        P(("blk", "grp"), None),
        P(),
        P(),
        P(),
        P(),
        P(("grp", "blk"), None, None),
        P(("grp", "blk")),
    )
    return jax.shard_map(
        per_device, mesh=mesh, in_specs=placed, out_specs=P("blk", None, "grp"), check_vma=False
    )
```

profile of v0, /device:TPU:8, one launch (start us, length us, event | category | flops | bytes accessed | tf_op | source)
XLA Modules:
  0.0 194.6 jit_solution(5666250183302063187)
XLA Ops:
  6.5 0.0 copy-start
  6.5 0.0 all-gather.3.cloned.1.call-start
  6.5 0.7 all-gather.3.cloned.1.call-update
  7.3 1.3 dynamic-slice.1
  8.5 1.3 dynamic-slice
  9.9 20.7 %all-gather = bf16[16,2,192]{2,1,0:T(2,128)(2,1)S(1)} all-gather(bf16[1,2,192]{2,1,0:T(2,128)(2,1)} %bitcast.30), channel_id=1, replica_groups=mesh['grp'=16,'blk'=32] {'grp'}, dimensions={0}, use_global_device_ids=true | all-gather | bytes 13056 | tf_op jit(solution)/shard_map/all_gather | solution.py:34
  32.0 0.9 dynamic-update-slice
  32.8 0.8 dynamic-update-slice.1
  33.7 8.5 %all-reduce = s32[32]{0:T(128)S(1)} all-reduce(s32[32]{0:T(128)S(1)} %dynamic-update-slice), channel_id=1, replica_groups=mesh['grp'=16,'blk'=32] {'grp'}, use_global_device_ids=true, to_apply=%add | all-reduce | flops 32 | bytes 256
  42.1 26.7 %all-reduce.1 = s32[256]{0:T(256)S(1)} all-reduce(s32[256]{0:T(256)S(1)} %dynamic-update-slice.1), channel_id=1, replica_groups=mesh['grp'=16,'blk'=32] {'blk'}, use_global_device_ids=true, to_apply=%add.1 | all-reduce | flops 256 | bytes 2048
  68.8 0.2 convolution_bitcast_fusion
  69.0 1.9 fusion.19
  70.9 0.8 multiply_convert_fusion
  71.7 34.7 %all_gather.15 = bf16[32,2,4000]{2,1,0:T(2,128)(2,1)S(1)} all-gather(bf16[2,2,4000]{2,1,0:T(2,128)(2,1)S(1)} %multiply_convert_fusion), channel_id=1, replica_groups=mesh['grp'=16,'blk'=32] {'grp'}, dimensions={0}, use_global_device_ids=true | all-gather | bytes 544000 | tf_op jit(solution)/shard_map/all_gather | solution.py:32
  106.4 0.0 copy-done
  106.4 1.9 fusion.34
  108.3 15.9 %all-gather.3.cloned.1.call-done = bf16[256,2,4000]{2,1,0:T(2,128)(2,1)} async-done(((bf16[8,2,4000]{2,1,0:T(2,128)(2,1)}), bf16[256,2,4000]{2,1,0:T(2,128)(2,1)}) %all-gather.3.cloned.1.call-update) | async-done | bytes 4096016 | tf_op jit(solution)/shard_map/all_gather | solution.py:45
  124.2 11.6 %fusion.33 = (bf16[256,1,4000]{2,1,0:T(2,128)(2,1)}, bf16[256,1,4000]{2,1,0:T(2,128)(2,1)}) fusion(bf16[256,2,4000]{2,1,0:T(2,128)(2,1)} %all-gather.3.cloned.1.call-done), kind=kLoop, calls=%fused_computation.37 | loop fusion | bytes 8192000 | tf_op jit(solution)/shard_map/slice | solution.py:47
  135.8 9.2 %copy.20 = bf16[256,1,4000]{0,2,1:T(8,128)(2,1)S(1)} copy(bf16[256,1,4000]{2,1,0:T(2,128)(2,1)} %get-tuple-element.7) | data formatting | bytes 4096000
  144.9 0.0 copy-start.2
  145.0 9.7 %copy.21 = bf16[256,1,4000]{0,2,1:T(8,128)(2,1)} copy(bf16[256,1,4000]{2,1,0:T(2,128)(2,1)} %get-tuple-element.8) | data formatting | bytes 4096000
  154.7 0.0 copy-done.2
  154.7 0.0 copy-start.1
  154.7 4.7 %fusion.4 = f32[64,256]{1,0:T(8,128)S(1)} fusion(f32[64,4000]{1,0:T(8,128)} %param.12, bf16[256,1,4000]{0,2,1:T(8,128)(2,1)S(1)} %copy.20, bf16[256,1,4000]{0,2,1:T(8,128)(2,1)} %copy.21, f32[4000]{0:T(1024)S(1)} %copy-done.2), kind=kOutput, calls=%fused_computation.6 | convolution fusion | flops 792064000 | bytes 5201536 | tf_op jit(solution)/shard_map/dot_general | solution.py:54
  159.4 0.0 copy-done.1
  159.4 0.6 bitcast_convert_fusion
  160.0 0.2 convolution_multiply_fusion
  160.2 13.2 %add_convert_fusion = (bf16[9,256,1,4000]{1,3,2,0:T(8,128)(2,1)}, bf16[9,256,1,4000]{1,3,2,0:T(8,128)(2,1)}) fusion(f32[256,4000]{0,1:T(8,128)S(1)} %get-tuple-element.12, f32[9,4000]{1,0:T(8,128)S(1)} %get-tuple-element.10, f32[256,4000]{0,1:T(8,128)S(1)} %get-tuple-element.13, f32[9,4000]{1,0:T(8,128)S(1)} %get-tuple-element.9), kind=kLoop, calls=%fused_computation.5 | loop fusion | flops 73728000 | bytes 45344000 | tf_op jit(solution)/shard_map/convert.2
  173.4 14.3 %fusion.14 = f32[32,9,256]{2,0,1:T(8,128)} fusion(bf16[9,256,1,4000]{1,3,2,0:T(8,128)(2,1)} %get-tuple-element.6, bf16[9,256,1,4000]{1,3,2,0:T(8,128)(2,1)} %get-tuple-element.5, bf16[32,2,4000]{2,1,0:T(2,128)(2,1)S(1)} %all_gather.15, f32[32,256]{1,0:T(8,128)S(1)} %convolution_bitcast_fusion, f32[32,256]{1,0:T(8,128)S(1)} %convolution_multiply_fusion), kind=kOutput, calls=%fused_computation.14 | convolution fusion | flops 1253523456 | bytes 37736448 | tf_op jit(solution)/shard_map/nck,tmck->ntm/dot_general | solution.py:52
  (3 shorter events, 0.0 us)
Async XLA Ops:
  6.5 99.9 %copy-start = (f32[9,4000]{1,0:T(8,128)S(1)}, f32[9,4000]{1,0:T(8,128)}, u32[]{:S(2)}) copy-start(f32[9,4000]{1,0:T(8,128)} %param.14) | copy-start | bytes 432004
  6.5 117.6 %all-gather.3.cloned.1.call-start = ((), (), s32[]{:S(2)}) async-start(), calls=%async_computation | async-start | bytes 4325376 | tf_op jit(solution)/shard_map/all_gather | solution.py:45
  144.9 9.7 %copy-start.2 = (f32[4000]{0:T(1024)S(1)}, f32[4000]{0:T(1024)}, u32[]{:S(2)}) copy-start(f32[4000]{0:T(1024)} %param.13) | copy-start | bytes 48004
  154.7 4.7 %copy-start.1 = (bf16[256,1,4000]{0,2,1:T(8,128)(2,1)S(1)}, bf16[256,1,4000]{0,2,1:T(8,128)(2,1)}, u32[]{:S(2)}) copy-start(bf16[256,1,4000]{0,2,1:T(8,128)(2,1)} %copy.21) | copy-start | bytes 6144004
Sparse Core Ops, SparseCore 0:
  10.5 113.6 all-gather.2
where the time goes:
time: 195 us
  blocking collectives  90.6 us (46%)
  local copies, waits for them, and re-layouts  34.8 us (18%)
  matrix products  23.2 us (12%)
  waiting for transfers between devices  16.6 us (9%)
  between operations  14.8 us (8%)
  other arithmetic  14.6 us (7%)
    unnamed x2, blocking collectives  35.2 us
    all_gather x1, blocking collectives, per_device(): lax.all_gather(local_weighted, 'grp', axis=0, tiled=True)  34.7 us
    unnamed x15, local copies, waits for them, and re-layouts  23.2 us
    all_gather x1, blocking collectives, per_device(): lax.all_gather(orient_prior, 'grp', axis=0, tiled=True)  20.7 us
    all_gather x1, waiting for transfers between devices, per_device(): bank = lax.all_gather(projections, 'blk', axis=0, tiled=True)  15.9 us
    dot_general x1, matrix products, per_device(): jnp.einsum('nck,tmck->ntm', weighted, shifted, preferred_element_type=jnp...  14.3 us
    another operation x1, other arithmetic  13.2 us
    slice x1, local copies, waits for them, and re-layouts, per_device(): bank_real = bank[:, 0, :].astype(jnp.float32)  11.6 us
  transfers between devices with their start and end apart: 1, of which 1 were waited for; matrix products, arithmetic and copies ran while one was open for 5% of the time, Pallas kernels for 0%

commit v1 on v0

v1 whole, which is shorter than its diff:
```python
import functools

import jax
import jax.numpy as jnp
from jax import lax
from jax.experimental import pallas as pl
from jax.experimental.pallas import tpu as pltpu
from jax.sharding import PartitionSpec as P

MESH = pl.DeviceIdType.MESH
NX, NZL, NC, NZH, NY = 4, 2, 2, 4, 8
NZ = NZH * NZL
NT = 9
PJ = 8
LANES = 128
KE = 33 * LANES
KH = 17 * LANES
PIECES = ((0, 8), (8, 8), (16, 8), (24, 9))
NJ = NY * PJ
NS = (NT * NJ + LANES - 1) // LANES
ROWS = NZ * NX * 8


def rem(a, n):
    return lax.rem(a, jnp.int32(n))


def div(a, n):
    return lax.div(a, jnp.int32(n))


def kernel(
    pc, wc, cosr, sinr, out,
    bank, wrecv, wbuf, sbuf, acc0, acc1, ebuf, rbuf,
    lsem, ysend, yrecv, zsend, zrecv, xsend, xrecv, psend, precv, csend, crecv, esend, erecv,
):
    grp = lax.axis_index("grp")
    blk = lax.axis_index("blk")
    x, zl, core = div(grp, 4), rem(div(grp, 2), 2), rem(grp, 2)
    zh, y = div(blk, 8), rem(blk, 8)
    z = zh * 2 + zl

    def dev(x_=x, z_=z, core_=core, y_=y):
        return ((x_ * 2 + rem(z_, 2)) * 2 + core_, div(z_, 2) * 8 + y_)

    partner = dev(core_=1 - core)
    yr, yl = dev(y_=rem(y + 1, NY)), dev(y_=rem(y + NY - 1, NY))
    zr, zlft = dev(z_=rem(z + 1, NZ)), dev(z_=rem(z + NZ - 1, NZ))
    xp = [dev(x_=rem(x + d, NX)) for d in (1, 2, 3)]
    ep = [dev(z_=rem(z + 2 * d, NZ)) for d in (1, 2, 3)]

    barrier = pltpu.get_barrier_semaphore()
    peers = [partner, yr, yl, zr, zlft] + xp + ep
    for p in peers:
        pl.semaphore_signal(barrier, inc=1, device_id=p, device_id_type=MESH)
    pl.semaphore_wait(barrier, len(peers))

    started = []

    def send(src, dst, ss, rs, to):
        c = pltpu.make_async_remote_copy(
            src_ref=src, dst_ref=dst, send_sem=ss, recv_sem=rs, device_id=to, device_id_type=MESH
        )
        c.start()
        started.append(c)

    def arrive(dst, ss, rs, frm):
        pltpu.make_async_remote_copy(
            src_ref=dst, dst_ref=dst, send_sem=ss, recv_sem=rs, device_id=frm, device_id_type=MESH
        ).wait_recv()

    def lanes(q):
        return pl.ds(PIECES[q][0] * LANES, PIECES[q][1] * LANES)

    def in_step(s, d, q):
        return s < 4 or (q < 2) == (d == 0)

    def y_send(s, q):
        for d, to in ((0, yr), (1, yl)):
            if in_step(s, d, q):
                y_send1(s, q, d, to)

    def y_send1(s, q, d, to):
        o = rem(y + (NY - (s - 1) if d == 0 else s - 1), NY)
        src = pc.at[:, lanes(q)] if s == 1 else bank.at[o, :, lanes(q)]
        send(src, bank.at[o, :, lanes(q)], ysend.at[d, s - 1, q], yrecv.at[d, s - 1, q], to)

    def y_step(s):
        for q in range(4):
            for d, to in ((0, yr), (1, yl)):
                if in_step(s, d, q):
                    o = rem(y + (NY - s if d == 0 else s), NY)
                    arrive(bank.at[o, :, lanes(q)], ysend.at[d, s - 1, q], yrecv.at[d, s - 1, q], to)
                    if s < 4 and in_step(s + 1, d, q):
                        y_send1(s + 1, q, d, to)

    def wblock(o, h=None):
        xs = slice(None) if h is None else pl.ds(2 * h, 2)
        return (div(o, 2), xs, rem(o, 2))

    def z_send(s, d):
        o = rem(z + (NZ - (s - 1) if d == 0 else s - 1), NZ)
        a, b, c = wblock(o, d if s == 4 else None)
        ref = wbuf.at[core, a, b, c]
        send(ref, ref, zsend.at[d, s - 1], zrecv.at[d, s - 1], zr if d == 0 else zlft)

    def p_send(s, d, o):
        a, b, c = wblock(o, d if s == 4 else None)
        ref = wbuf.at[core, a, b, c]
        send(ref, ref, psend.at[d, s], precv.at[d, s], partner)

    def p_wait(s, d, o):
        a, b, c = wblock(o, d if s == 4 else None)
        arrive(wbuf.at[1 - core, a, b, c], psend.at[d, s], precv.at[d, s], partner)

    def z_origin(s, d):
        return rem(z + (NZ - s if d == 0 else s), NZ)

    def z_step(s):
        for d in (0, 1):
            o = z_origin(s, d)
            a, b, c = wblock(o, d if s == 4 else None)
            arrive(wbuf.at[core, a, b, c], zsend.at[d, s - 1], zrecv.at[d, s - 1], zr)
            if s < 4:
                z_send(s + 1, d)
            p_send(s, d, o)

    def shift_tiles(first, count):
        def body(i, carry):
            at = pl.ds(pl.multiple_of(i * LANES, LANES), LANES)
            real, imag = [], []
            for yy in range(NY):
                both = bank[yy, :, at].astype(jnp.float32)
                real.append(both[:PJ])
                imag.append(both[PJ:])
            for t in range(NT):
                c = jnp.broadcast_to(cosr[pl.ds(t, 1), at], (PJ, LANES))
                s = jnp.broadcast_to(sinr[pl.ds(t, 1), at], (PJ, LANES))
                for m in range(0, NY, 2):
                    r0 = c * real[m] + s * imag[m]
                    r1 = c * real[m + 1] + s * imag[m + 1]
                    i0 = c * imag[m] - s * real[m]
                    i1 = c * imag[m + 1] - s * real[m + 1]
                    rows = pl.ds(t * NJ + m * PJ, 2 * PJ)
                    sbuf[0, rows, at] = jnp.concatenate([r0, r1], axis=0).astype(jnp.bfloat16)
                    sbuf[1, rows, at] = jnp.concatenate([i0, i1], axis=0).astype(jnp.bfloat16)
            return carry

        lax.fori_loop(first, first + count, body, 0)

    local = pltpu.make_async_copy(pc, bank.at[y], lsem)
    local.start()
    send(wc.at[1 - core], wrecv, csend, crecv, partner)
    for q in range(4):
        y_send(1, q)
    arrive(wrecv, csend, crecv, partner)
    mine = wc[core].astype(jnp.float32)
    theirs = wrecv[...].astype(jnp.float32)
    first = jnp.where(core == 0, mine, theirs)
    second = jnp.where(core == 0, theirs, mine)
    wbuf[core, zh, x, zl] = jnp.concatenate([first, second], axis=0).astype(jnp.bfloat16)
    own = wbuf.at[core, zh, x, zl]
    for d in range(3):
        send(own, own, xsend.at[d], xrecv.at[d], xp[d])
    y_step(1)
    for d in range(3):
        arrive(wbuf.at[core, zh, rem(x + NX - 1 - d, NX), zl], xsend.at[d], xrecv.at[d], xp[d])
    z_send(1, 0)
    z_send(1, 1)
    p_send(0, 0, z)
    y_step(2)
    z_step(1)
    y_step(3)
    z_step(2)
    y_step(4)
    local.wait()
    shift_tiles(0, 16)
    z_step(3)
    shift_tiles(16, 17)
    z_step(4)
    p_wait(0, 0, z)
    for s in range(1, 5):
        for d in (0, 1):
            p_wait(s, d, z_origin(s, d))

    dims = (((1,), (1,)), ((), ()))
    for part, acc in ((0, acc0), (1, acc1)):
        fresh = True
        for kh, lo, n, base in ((0, 0, 8, 0), (0, 8, 8, 0), (1, 0, 8, 16), (1, 8, 9, 16)):
            w = wbuf[kh, :, :, :, :, pl.ds(lo * LANES, n * LANES)].reshape(ROWS, n * LANES)
            sh = sbuf[part, :, pl.ds((base + lo) * LANES, n * LANES)]
            prod = lax.dot_general(w, sh, dims, preferred_element_type=jnp.float32)
            tail = jnp.zeros((ROWS, NS * LANES - NT * NJ), jnp.float32)
            prod = jnp.concatenate([prod, tail], axis=1)
            for n in range(NS):
                slab = prod[:, n * LANES : (n + 1) * LANES]
                acc[n] = slab if fresh else acc[n] + slab
            fresh = False

    for d in (2, 1, 3, 0):
        o = rem(zh + d, NZH)
        for n in range(NS):
            val = acc0[n, pl.ds(o * 64, 32, stride=2), :] + acc1[n, pl.ds(o * 64 + 1, 32, stride=2), :]
            if d == 0:
                rbuf[zh, n] = val
            else:
                ebuf[d - 1, n] = val
        if d:
            send(ebuf.at[d - 1], rbuf.at[zh], esend.at[d - 1], erecv.at[d - 1], ep[d - 1])
    for d in (1, 3, 2):
        arrive(rbuf.at[rem(zh + NZH - d, NZH)], esend.at[d - 1], erecv.at[d - 1], ep[d - 1])
    for t in range(NT):
        slab, col = t // 2, pl.ds(t % 2 * NJ, NJ)
        for m in range(0, NZH, 2):
            out[t, :, pl.ds(m * NJ, 2 * NJ)] = jnp.concatenate(
                [rbuf[m, slab, :, col], rbuf[m + 1, slab, :, col]], axis=1
            )
    for c in started:
        c.wait_send()


def split3(v):
    hi = lax.reduce_precision(v, 8, 7)
    mid = lax.reduce_precision(v - hi, 8, 7)
    lo = v - hi - mid
    return hi.astype(jnp.bfloat16), mid.astype(jnp.bfloat16), lo.astype(jnp.bfloat16)


def per_device(
    particles,
    ctf_class,
    orient_prior,
    ctf_curves,
    noise_weight,
    shift_phase,
    trans_index,
    projections,
    orient_subset,
):
    highest = lax.Precision.HIGHEST
    bf16 = jnp.bfloat16
    nclass = ctf_curves.shape[0]
    nsub = orient_prior.shape[1]
    k = ctf_curves.shape[1]
    half = nsub // 2

    def onehot(ids, n, dtype):
        return (ids[:, None] == jnp.arange(n, dtype=jnp.int32)[None, :]).astype(dtype)

    weight_rows = ctf_curves * noise_weight[None, :]
    curve_sq = weight_rows * ctf_curves
    hot = onehot(ctf_class, nclass, jnp.float32)
    curve = jnp.dot(hot, weight_rows, precision=highest)
    weighted = (particles.astype(jnp.float32) * curve[:, None, :]).astype(bf16)
    hotb = hot.astype(bf16)
    none = jnp.zeros_like(hotb)
    wext = jnp.stack(
        [
            jnp.concatenate([orient_prior[:, :half], hotb, hotb], axis=1),
            jnp.concatenate([orient_prior[:, half:], hotb, none], axis=1),
        ],
        axis=1,
    )
    wfull = jnp.concatenate([weighted, wext], axis=2).reshape(4, KE)
    wc = jnp.stack([wfull[:, :KH], wfull[:, KE - KH :]], axis=0)

    real = projections[:, 0, :].astype(jnp.float32)
    imag = projections[:, 1, :].astype(jnp.float32)
    power = real * real + imag * imag
    norm = -0.5 * lax.dot_general(power, curve_sq, (((1,), (1,)), ((), ())), precision=highest)
    hi, mid, lo = split3(norm)
    sub = onehot(orient_subset, nsub, bf16)
    pext = jnp.concatenate(
        [
            jnp.concatenate([sub[:, :half], hi, mid], axis=1),
            jnp.concatenate([sub[:, half:], lo, jnp.zeros_like(lo)], axis=1),
        ],
        axis=0,
    )
    pc = jnp.concatenate(
        [jnp.concatenate([projections[:, 0, :], projections[:, 1, :]], axis=0), pext], axis=1
    )

    pick = onehot(trans_index, shift_phase.shape[0], jnp.float32)
    angle = jnp.dot(pick, shift_phase, precision=highest)
    angle = jnp.pad(angle, ((0, 0), (0, KE - k)))
    cosr, sinr = jnp.cos(angle), jnp.sin(angle)

    dma = pltpu.SemaphoreType.DMA
    vm = pl.BlockSpec(memory_space=pltpu.VMEM)
    scores = pl.pallas_call(
        kernel,
        out_shape=jax.ShapeDtypeStruct((NT, 32, NZH * NJ), jnp.float32),
        in_specs=[vm] * 4,
        out_specs=vm,
        scratch_shapes=[
            pltpu.VMEM((NY, 2 * PJ, KE), bf16),
            pltpu.VMEM((4, KH), bf16),
            pltpu.VMEM((2, NZH, NX, NZL, 8, KH), bf16),
            pltpu.VMEM((2, NT * NJ, KE), bf16),
            pltpu.VMEM((NS, ROWS, LANES), jnp.float32),
            pltpu.VMEM((NS, ROWS, LANES), jnp.float32),
            pltpu.VMEM((3, NS, 32, LANES), jnp.float32),
            pltpu.VMEM((NZH, NS, 32, LANES), jnp.float32),
            dma,
            dma((2, 4, 4)),
            dma((2, 4, 4)),
            dma((2, 4)),
            dma((2, 4)),
            dma((3,)),
            dma((3,)),
            dma((2, 5)),
            dma((2, 5)),
            dma,
            dma,
            dma((3,)),
            dma((3,)),
        ],
        compiler_params=pltpu.CompilerParams(
            collective_id=0, has_side_effects=True, vmem_limit_bytes=48 << 20
        ),
        name="scores",
    )(pc, wc, cosr, sinr)
    return jnp.transpose(scores, (1, 0, 2))


def solution(mesh):
    placed = (
        P(("blk", "grp"), None, None),
        P(("blk", "grp")),
        P(("blk", "grp"), None),
        P(),
        P(),
        P(),
        P(),
        P(("grp", "blk"), None, None),
        P(("grp", "blk")),
    )
    return jax.shard_map(
        per_device, mesh=mesh, in_specs=placed, out_specs=P("blk", None, "grp"), check_vma=False
    )
```

time: 195 us -> 60.9 us (0.31)
  the two profiles are of different devices: /device:TPU:8 before, /device:TPU:17 now
where the time goes in v1:
time: 60.9 us; the launch traced here: 60.7 us
  Pallas kernels  52 us (85%)
  local copies, waits for them, and re-layouts  4.43 us (7%)
  matrix products  2.98 us (5%)
  other arithmetic  1.16 us (2%)
    pallas_call x1, Pallas kernels, per_device(): pl.pallas_call(kernel, out_shape=jax.ShapeDtypeStruct((NT, 32, NZH * NJ),...  52 us
    unnamed x19, local copies, waits for them, and re-layouts  2.76 us
    dot_general x1, matrix products, per_device(): curve = jnp.dot(hot, weight_rows, precision=highest)  1.74 us

profile of v1, /device:TPU:17, one launch (start us, length us, event | category | flops | bytes accessed | tf_op | source)
XLA Modules:
  0.0 60.7 jit_solution(1243207660139930714)
XLA Ops:
  0.0 0.0 copy-start
  0.0 0.8 %convert_convert_fusion = bf16[2,64]{1,0:T(2,128)(2,1)S(1)} fusion(s32[2]{0:T(128)} %param.10), kind=kLoop, calls=%fused_computation.34 | loop fusion | flops 384 | bytes 264 | tf_op jit(solution)/shard_map/convert_element_type | solution.py:255
  0.8 0.0 copy-start.5
  0.8 0.1 pad.13.clone
  0.9 0.6 copy-done.5
  1.5 0.1 fusion.16
  1.5 0.0 copy-start.8
  1.5 0.0 copy-start.3
  1.5 0.1 maximum_bitcast_fusion
  1.6 0.6 copy-done.8
  2.2 0.1 fusion.9
  2.3 0.1 fusion.15
  2.3 0.0 copy-start.6
  2.3 0.0 copy-done.3
  2.3 0.7 %copy-done.6 = s32[2]{0:T(128)S(1)} copy-done((s32[2]{0:T(128)S(1)}, s32[2]{0:T(128)}, u32[]{:S(2)}) %copy-start.6) | copy-done | bytes 32
  3.0 0.0 copy-start.4
  3.0 0.0 copy-start.7
  3.0 0.0 copy-start.2
  3.0 1.7 %fusion = f32[2,4000]{1,0:T(2,128)S(1)} fusion(f32[64,4000]{1,0:T(8,128)} %param.12, f32[4000]{0:T(1024)S(1)} %copy-done.3, s32[2]{0:T(128)S(1)} %copy-done.6), kind=kOutput, calls=%fused_computation | convolution fusion | flops 6400128 | bytes 1072008 | tf_op jit(solution)/shard_map/dot_general | solution.py:253
  4.7 0.0 copy-done.4
  4.7 0.0 copy-start.1
  4.8 0.1 pad_maximum_fusion.1
  4.9 0.1 reshape.8
  5.0 0.0 copy-done
  5.0 0.0 copy-done.7
  5.0 0.3 fusion.10
  5.4 0.0 copy-done.2
  5.4 0.2 fusion.14
  5.6 0.2 copy_bitcast_fusion
  5.8 0.2 copy-done.1
  6.0 0.9 %reduce-precision_convert_fusion.1 = (bf16[8,64]{1,0:T(8,128)(2,1)S(1)}, bf16[8,64]{1,0:T(8,128)(2,1)S(1)}, bf16[8,64]{1,0:T(8,128)(2,1)S(1)}) fusion(f32[64,4000]{1,0:T(8,128)S(1)} %copy-done.1, f32[4000]{0:T(1024)S(1)} %copy-done.3, bf16[8,4000]{1,0:T(8,128)(2,1)S(1)} %get-tuple-element.20, bf16[8,4000]{1,0:T(8,128)(2,1)S(1)} %get-tuple-element.21), kind=kOutput, calls=%fused_computation.28 | convolution fusion | flops 25252096 | bytes 1171072 | tf_op jit(solution)/shard_map/dot_general | solution.py:270
  6.9 0.1 maximum_maximum_fusion.pc
  7.0 1.0 %pad_sine_fusion = (f32[9,4224]{1,0:T(8,128)S(1)}, f32[9,4224]{1,0:T(8,128)S(1)}) fusion(f32[9,4000]{1,0:T(8,128)S(1)} %fusion.10), kind=kLoop, calls=%fused_computation.6 | loop fusion | bytes 448128 | tf_op jit(solution)/shard_map/sin | solution.py:287
  8.0 52.0 %scores.1 = f32[9,32,256]{2,1,0:T(8,128)S(1)} custom-call(bf16[16,4224]{1,0:T(8,128)(2,1)S(1)} %maximum_maximum_fusion.pc, bf16[2,4,2176]{2,1,0:T(4,128)(2,1)S(1)} %pad_maximum_fusion.wc, f32[9,4224]{1,0:T(8,128)S(1)} %get-tuple-element.6.cosr, f32[9,4224]{1,0:T(8,128)S(1)} %get-tuple-element.5.sinr), custom_call_target="tpu_custom_call" | custom-call | tf_op jit(solution)/shard_map/scores/pallas_call | solution.py:291
  59.9 0.7 %copy.18 = f32[32,9,256]{2,0,1:T(8,128)} copy(f32[32,9,256]{2,0,1:T(8,128)S(1)} %bitcast.14) | data formatting | bytes 589824
  (7 shorter events, 0.1 us)
Async XLA Ops:
  0.0 5.0 %copy-start = (f32[9,4000]{1,0:T(8,128)S(1)}, f32[9,4000]{1,0:T(8,128)}, u32[]{:S(2)}) copy-start(f32[9,4000]{1,0:T(8,128)} %param.14) | copy-start | bytes 432004
  0.8 0.7 %copy-start.5 = (bf16[2,192]{1,0:T(2,128)(2,1)S(1)}, bf16[2,192]{1,0:T(2,128)(2,1)}, u32[]{:S(2)}) copy-start(bf16[2,192]{1,0:T(2,128)(2,1)} %param.11) | copy-start | bytes 2308
  1.5 0.7 %copy-start.8 = (s32[8]{0:T(128)S(1)}, s32[8]{0:T(128)}, u32[]{:S(2)}) copy-start(s32[8]{0:T(128)} %param.17) | copy-start | bytes 100
  1.5 0.8 %copy-start.3 = (f32[4000]{0:T(1024)S(1)}, f32[4000]{0:T(1024)}, u32[]{:S(2)}) copy-start(f32[4000]{0:T(1024)} %param.13) | copy-start | bytes 48004
  2.3 0.7 %copy-start.6 = (s32[2]{0:T(128)S(1)}, s32[2]{0:T(128)}, u32[]{:S(2)}) copy-start(s32[2]{0:T(128)} %param.10) | copy-start | bytes 28
  3.0 1.8 %copy-start.4 = (bf16[2,2,4000]{2,1,0:T(2,128)(2,1)S(1)}, bf16[2,2,4000]{2,1,0:T(2,128)(2,1)}, u32[]{:S(2)}) copy-start(bf16[2,2,4000]{2,1,0:T(2,128)(2,1)} %param.9) | copy-start | bytes 96004
  3.0 2.0 %copy-start.7 = (s32[9]{0:T(128)S(1)}, s32[9]{0:T(128)}, u32[]{:S(2)}) copy-start(s32[9]{0:T(128)} %param.15) | copy-start | bytes 112
  3.0 2.4 %copy-start.2 = (bf16[8,2,4000]{2,1,0:T(2,128)(2,1)S(1)}, bf16[8,2,4000]{2,1,0:T(2,128)(2,1)}, u32[]{:S(2)}) copy-start(bf16[8,2,4000]{2,1,0:T(2,128)(2,1)} %param.16) | copy-start | bytes 384004
  4.7 1.2 %copy-start.1 = (f32[64,4000]{1,0:T(8,128)S(1)}, f32[64,4000]{1,0:T(8,128)}, u32[]{:S(2)}) copy-start(f32[64,4000]{1,0:T(8,128)} %param.12) | copy-start | bytes 3072004

commit v2 on v0

v2 whole, which is shorter than its diff:
```python
import jax
import jax.numpy as jnp
from jax import lax
from jax.experimental import pallas as pl
from jax.experimental.pallas import tpu as pltpu
from jax.sharding import PartitionSpec as P

MESH = pl.DeviceIdType.MESH
NX, NZL, NC, NZH, NY = 4, 2, 2, 4, 8
NZ = NZH * NZL
NT = 9
PJ = 8
LANES = 128
KE = 33 * LANES
KH = 17 * LANES
MAIN = 31
PIECES = ((0, 10), (10, 10), (20, 11), (31, 2))
NQ = len(PIECES)
NJ = NY * PJ
NS = 5
NJ = NY * PJ
EARLY, LATE = (7, 0, 1), (2, 3, 4, 5, 6)
GROUPS = ((EARLY, 0, 2), (LATE, 2, 3))
ROWS = NZ * NX * 8


def rem(a, n):
    return lax.rem(a, jnp.int32(n))


def div(a, n):
    return lax.div(a, jnp.int32(n))


def kernel(
    cls, tri, sub, pc, wp, prior, curves, weight, phase, out,
    bank, wloc, wrecv, wbuf, cosr, sinr, sbuf, acc0, acc1, ebuf, rbuf,
    lsem, ysend, yrecv, zsend, zrecv, xsend, xrecv, psend, precv, hsend, hrecv, csend, crecv, esend, erecv,
):
    grp = lax.axis_index("grp")
    blk = lax.axis_index("blk")
    x, zl, core = div(grp, 4), rem(div(grp, 2), 2), rem(grp, 2)
    zh, y = div(blk, 8), rem(blk, 8)
    z = zh * 2 + zl

    def dev(x_=x, z_=z, core_=core, y_=y):
        return ((x_ * 2 + rem(z_, 2)) * 2 + core_, div(z_, 2) * 8 + y_)

    partner = dev(core_=1 - core)
    yr, yl = dev(y_=rem(y + 1, NY)), dev(y_=rem(y + NY - 1, NY))
    zr, zlft = dev(z_=rem(z + 1, NZ)), dev(z_=rem(z + NZ - 1, NZ))
    xp = [dev(x_=rem(x + d, NX)) for d in (1, 2, 3)]
    ep = [dev(z_=rem(z + 2 * d, NZ)) for d in (1, 2, 3)]

    barrier = pltpu.get_barrier_semaphore()
    peers = [partner, yr, yl, zr, zlft] + xp
    for p in peers:
        pl.semaphore_signal(barrier, inc=1, device_id=p, device_id_type=MESH)

    f32, bf16 = jnp.float32, jnp.bfloat16
    k = curves.shape[1]
    first_rows = lax.broadcasted_iota(jnp.int32, (4, 1), 0) < 2
    nothing = jnp.zeros((1, (MAIN + 1) * LANES - k), f32)

    def curve_row(p):
        total = jnp.zeros((8, k), f32)
        for g in range(curves.shape[0] // 8):
            chosen = lax.broadcasted_iota(jnp.int32, (8, 1), 0) + 8 * g == cls[p]
            total = jnp.where(chosen, curves[pl.ds(8 * g, 8), :], total)
        row = jnp.sum(total, axis=0, keepdims=True)
        return jnp.concatenate([row * weight[...], nothing], axis=1)

    scaled = wp[...].astype(f32) * jnp.where(first_rows, curve_row(0), curve_row(1))
    lane4 = lax.broadcasted_iota(jnp.int32, (4, LANES), 1)
    part4 = lax.broadcasted_iota(jnp.int32, (4, LANES), 0) % 2
    own_class = jnp.where(first_rows, cls[0], cls[1])
    hit = (lane4 == own_class) | ((lane4 == own_class + 64) & (part4 == 0))
    wide = jnp.concatenate(
        [
            scaled[:, : MAIN * LANES],
            scaled[:, MAIN * LANES :] + prior[...].astype(f32),
            jnp.where(hit, 1.0, 0.0),
        ],
        axis=1,
    ).astype(bf16)
    wloc[0] = wide[:, :KH]
    wloc[1] = wide[:, KE - KH :]
    pl.semaphore_wait(barrier, len(peers))

    started = []

    def send(src, dst, ss, rs, to):
        c = pltpu.make_async_remote_copy(
            src_ref=src, dst_ref=dst, send_sem=ss, recv_sem=rs, device_id=to, device_id_type=MESH
        )
        c.start()
        started.append(c)

    def arrive(dst, ss, rs, frm):
        pltpu.make_async_remote_copy(
            src_ref=dst, dst_ref=dst, send_sem=ss, recv_sem=rs, device_id=frm, device_id_type=MESH
        ).wait_recv()

    def lanes(q):
        return pl.ds(PIECES[q][0] * LANES, PIECES[q][1] * LANES)

    def in_step(s, d, q):
        return s < 4 or (q < NQ // 2) == (d == 0)

    def y_send(s, q):
        for d, to in ((0, yr), (1, yl)):
            if in_step(s, d, q):
                y_send1(s, q, d, to)

    def slot(s, d):
        return (NY - s) % NY if d == 0 else s

    def y_send1(s, q, d, to):
        src = (bank.at[slot(s - 1, d)] if s > 1 or q == NQ - 1 else pc).at[:, lanes(q)]
        send(src, bank.at[slot(s, d), :, lanes(q)], ysend.at[d, s - 1, q], yrecv.at[d, s - 1, q], to)

    def y_step(s, pieces=range(NQ)):
        for q in pieces:
            for d, to in ((0, yr), (1, yl)):
                if in_step(s, d, q):
                    arrive(
                        bank.at[slot(s, d), :, lanes(q)],
                        ysend.at[d, s - 1, q], yrecv.at[d, s - 1, q], to,
                    )
                    if s < 4 and in_step(s + 1, d, q):
                        y_send1(s + 1, q, d, to)

    def at_x(g):
        return rem(x + g + NX, NX)

    def unit_a(half, o, g):
        return wbuf.at[half, div(o, 2), at_x(-g), rem(o, 2)]

    def plane_a(half, o):
        return wbuf.at[half, div(o, 2), :, rem(o, 2)]

    def z_origin(s, d):
        return rem(z + (NZ - s if d == 0 else s), NZ)

    def z_send(s, d, g):
        if s < 4 or (g < 2) == (d == 0):
            ref = unit_a(core, z_origin(s - 1, d), g)
            send(ref, ref, zsend.at[d, s - 1, g], zrecv.at[d, s - 1, g], zr if d == 0 else zlft)

    def z_step(s):
        for g in range(NX):
            for d in (0, 1):
                if s < 4 or (g < 2) == (d == 0):
                    ref = unit_a(core, z_origin(s, d), g)
                    arrive(ref, zsend.at[d, s - 1, g], zrecv.at[d, s - 1, g], zr)
                    if s < 4:
                        z_send(s + 1, d, g)
                    else:
                        send(ref, ref, hsend.at[g], hrecv.at[g], partner)
        if s < 4:
            for d in (0, 1):
                p_send(s, d)

    def p_send(s, d):
        ref = plane_a(core, z_origin(s, d))
        send(ref, ref, psend.at[d, s], precv.at[d, s], partner)

    def p_wait(s, d):
        arrive(plane_a(1 - core, z_origin(s, d)), psend.at[d, s], precv.at[d, s], partner)

    def shift(slot0):
        def body(i, carry):
            at = pl.ds(pl.multiple_of(i * LANES, LANES), LANES)
            both = [bank[slot0 + c, :, at].astype(f32) for c in (0, 1)]
            for t in range(NT):
                cos = jnp.broadcast_to(cosr[pl.ds(t, 1), at], (PJ, LANES))
                sin = jnp.broadcast_to(sinr[pl.ds(t, 1), at], (PJ, LANES))
                rows = pl.ds(t * NJ + slot0 * PJ, 2 * PJ)
                real = [cos * b[:PJ] + sin * b[PJ:] for b in both]
                imag = [cos * b[PJ:] - sin * b[:PJ] for b in both]
                sbuf[0, rows, at] = jnp.concatenate(real, axis=0).astype(bf16)
                sbuf[1, rows, at] = jnp.concatenate(imag, axis=0).astype(bf16)
            return carry

        lax.fori_loop(0, KE // LANES, body, 0)

    send(wloc.at[1 - core], wrecv, csend, crecv, partner)
    for q in range(NQ - 1):
        y_send(1, q)
    local = pltpu.make_async_copy(
        pc.at[:, pl.ds(0, MAIN * LANES)], bank.at[0, :, pl.ds(0, MAIN * LANES)], lsem
    )
    local.start()
    arrive(wrecv, csend, crecv, partner)
    mine = wloc[core].astype(jnp.float32)
    theirs = wrecv[...].astype(jnp.float32)
    first = jnp.where(core == 0, mine, theirs)
    second = jnp.where(core == 0, theirs, mine)
    wbuf[core, zh, x, zl] = jnp.concatenate([first, second], axis=0).astype(jnp.bfloat16)
    own = unit_a(core, z, 0)
    for d in range(3):
        send(own, own, xsend.at[d], xrecv.at[d], xp[d])
    for d in (0, 1):
        z_send(1, d, 0)
    both = pc[...].astype(f32)
    power = both[:PJ] * both[:PJ] + both[PJ:] * both[PJ:]
    curve_sq = curves[...] * weight[...] * curves[...]
    norm = -0.5 * lax.dot_general(
        power[:, :k], curve_sq, (((1,), (1,)), ((), ())),
        precision=lax.Precision.HIGHEST, preferred_element_type=f32,
    )
    high = norm.astype(bf16).astype(f32)
    mid = (norm - high).astype(bf16).astype(f32)
    low = norm - high - mid
    lane16 = lax.broadcasted_iota(jnp.int32, (2 * PJ, LANES), 1)
    row16 = lax.broadcasted_iota(jnp.int32, (2 * PJ, 1), 0)
    target = jnp.zeros((2 * PJ, 1), jnp.int32)
    for j in range(PJ):
        target = jnp.where(row16 == j, sub[j] + 32, target)
        target = jnp.where(row16 == PJ + j, sub[j] - 64, target)
    subset = jnp.where((lane16 == target) & (lane16 >= 32), 1.0, 0.0)
    bank[0, :, pl.ds(MAIN * LANES, LANES)] = (both[:, MAIN * LANES :] + subset).astype(bf16)
    terms = jnp.concatenate(
        [
            jnp.concatenate([high, mid], axis=1),
            jnp.concatenate([low, jnp.zeros_like(low)], axis=1),
        ],
        axis=0,
    )
    bank[0, :, pl.ds((MAIN + 1) * LANES, LANES)] = terms.astype(bf16)
    y_send(1, NQ - 1)
    y_step(1, range(NQ - 1))
    table = jnp.concatenate([phase[...], jnp.zeros((NT, KE - k), f32)], axis=1)
    row9 = lax.broadcasted_iota(jnp.int32, (NT, 1), 0)
    wanted = jnp.zeros((NT, 1), jnp.int32)
    for t in range(NT):
        wanted = jnp.where(row9 == t, tri[t], wanted)
    angle = jnp.zeros((NT, KE), f32)
    for t in range(NT):
        angle = jnp.where(wanted == t, table[t : t + 1], angle)
    cosr[...] = jnp.cos(angle)
    sinr[...] = jnp.sin(angle)
    y_step(1, (NQ - 1,))
    for g in range(1, NX):
        arrive(unit_a(core, z, g), xsend.at[g - 1], xrecv.at[g - 1], xp[g - 1])
        z_send(1, 0, g)
        z_send(1, 1, g)
    p_send(0, 0)
    z_step(1)
    local.wait()
    shift(0)
    y_step(2)
    z_step(2)
    shift(6)
    y_step(3)
    z_step(3)
    shift(2)
    y_step(4)
    shift(4)
    p_wait(0, 0)
    for s in range(1, 4):
        for d in (0, 1):
            p_wait(s, d)

    dims = (((1,), (1,)), ((), ()))

    def cross(part, acc, blocks):
        fresh = True
        for kh, first, tiles, base in ((0, 0, 8, 0), (0, 8, 8, 0), (1, 0, 8, 16), (1, 8, 9, 16)):
            at = pl.ds(first * LANES, tiles * LANES)
            w = [
                wbuf[kh, rem(zh + d, NZH), :, :, :, at].reshape(ROWS // NZH, tiles * LANES)
                for d in blocks
            ]
            w = jnp.concatenate(w, axis=0) if len(w) > 1 else w[0]
            sh = sbuf[part, :, pl.ds((base + first) * LANES, tiles * LANES)]
            prod = lax.dot_general(w, sh, dims, preferred_element_type=f32)
            fill = jnp.zeros((prod.shape[0], NS * LANES - NT * NJ), f32)
            prod = jnp.concatenate([prod, fill], axis=1)
            for m in range(NS):
                for n, d in enumerate(blocks):
                    slab = prod[n * 64 : (n + 1) * 64, m * LANES : (m + 1) * LANES]
                    rows = pl.ds(d * 64, 64)
                    acc[m, rows, :] = slab if fresh else acc[m, rows, :] + slab
            fresh = False

    def finish(blocks):
        cross(0, acc0, blocks)
        cross(1, acc1, blocks)
        for d in blocks:
            for m in range(NS):
                val = (
                    acc0[m, pl.ds(d * 64, 32, stride=2), :]
                    + acc1[m, pl.ds(d * 64 + 1, 32, stride=2), :]
                )
                if d == 0:
                    rbuf[zh, m] = val
                else:
                    ebuf[d - 1, m] = val
            if d:
                send(ebuf.at[d - 1], rbuf.at[zh], esend.at[d - 1], erecv.at[d - 1], ep[d - 1])

    finish((1, 3, 0))
    z_step(4)
    for g in range(NX):
        arrive(unit_a(1 - core, z_origin(4, 0), g), hsend.at[g], hrecv.at[g], partner)
    finish((2,))

    left = lax.broadcasted_iota(jnp.int32, (32, LANES), 1) < NJ

    def turned(m):
        for slab in range(NS):
            val = rbuf[m, slab]
            swapped = pltpu.roll(val, NJ, 1)
            yield pltpu.roll(jnp.where(left, val, swapped), PJ * y, 1)
            yield pltpu.roll(jnp.where(left, swapped, val), PJ * y, 1)

    for d in (1, 3, 2):
        arrive(rbuf.at[rem(zh + NZH - d, NZH)], esend.at[d - 1], erecv.at[d - 1], ep[d - 1])
    for m in range(0, NZH, 2):
        for t, low, high in zip(range(NT), turned(m), turned(m + 1)):
            out[t, :, pl.ds(m * NJ, LANES)] = jnp.where(left, low, high)
    for c in started:
        c.wait_send()


def per_device(
    particles,
    ctf_class,
    orient_prior,
    ctf_curves,
    noise_weight,
    shift_phase,
    trans_index,
    projections,
    orient_subset,
):
    f32, bf16 = jnp.float32, jnp.bfloat16
    k = ctf_curves.shape[1]
    fill = (MAIN + 1) * LANES - k
    pc = jnp.concatenate([projections[:, 0, :], projections[:, 1, :]], axis=0)
    pc = jnp.pad(pc, ((0, 0), (0, fill)))
    wp = jnp.pad(particles.reshape(4, k), ((0, 0), (0, fill)))
    prior = jnp.pad(orient_prior.reshape(4, fill), ((0, 0), (LANES - fill, 0)))

    dma = pltpu.SemaphoreType.DMA
    vm = pl.BlockSpec(memory_space=pltpu.VMEM)
    sm = pl.BlockSpec(memory_space=pltpu.SMEM)
    scores = pl.pallas_call(
        kernel,
        out_shape=jax.ShapeDtypeStruct((NT, 32, NZH * NJ), f32),
        in_specs=[sm] * 3 + [vm] * 6,
        out_specs=vm,
        scratch_shapes=[
            pltpu.VMEM((NY, 2 * PJ, KE), bf16),
            pltpu.VMEM((2, 4, KH), bf16),
            pltpu.VMEM((4, KH), bf16),
            pltpu.VMEM((2, NZH, NX, NZL, 8, KH), bf16),
            pltpu.VMEM((NT, KE), f32),
            pltpu.VMEM((NT, KE), f32),
            pltpu.VMEM((2, NT * NJ, KE), bf16),
            pltpu.VMEM((NS, ROWS, LANES), f32),
            pltpu.VMEM((NS, ROWS, LANES), f32),
            pltpu.VMEM((3, NS, 32, LANES), f32),
            pltpu.VMEM((NZH, NS, 32, LANES), f32),
            dma,
            dma((2, 4, NQ)),
            dma((2, 4, NQ)),
            dma((2, 4, NX)),
            dma((2, 4, NX)),
            dma((3,)),
            dma((3,)),
            dma((2, 4)),
            dma((2, 4)),
            dma((NX,)),
            dma((NX,)),
            dma,
            dma,
            dma((3,)),
            dma((3,)),
        ],
        compiler_params=pltpu.CompilerParams(
            collective_id=0, has_side_effects=True, vmem_limit_bytes=48 << 20
        ),
        name="scores",
    )(
        ctf_class, trans_index, orient_subset,
        pc, wp, prior, ctf_curves, noise_weight[None, :], shift_phase,
    )
    return jnp.transpose(scores, (1, 0, 2))


def solution(mesh):
    placed = (
        P(("blk", "grp"), None, None),
        P(("blk", "grp")),
        P(("blk", "grp"), None),
        P(),
        P(),
        P(),
        P(),
        P(("grp", "blk"), None, None),
        P(("grp", "blk")),
    )
    return jax.shard_map(
        per_device, mesh=mesh, in_specs=placed, out_specs=P("blk", None, "grp"), check_vma=False
    )
```

time: 195 us -> 56.2 us (0.29)
  the two profiles are of different devices: /device:TPU:8 before, /device:TPU:25 now
where the time goes in v2:
time: 56.2 us; the launch traced here: 55.9 us
  Pallas kernels  50.5 us (90%)
  local copies, waits for them, and re-layouts  5.3 us (9%)
    pallas_call x1, Pallas kernels, per_device(): pl.pallas_call(kernel, out_shape=jax.ShapeDtypeStruct((NT, 32, NZH * NJ),...  50.5 us
    unnamed x13, local copies, waits for them, and re-layouts  2.17 us
    slice x1, local copies, waits for them, and re-layouts, per_device(): pc = jnp.concatenate([projections[:, 0, :], projections[:, 1, :]], axis=0)  1.25 us

profile of v2, /device:TPU:25, one launch (start us, length us, event | category | flops | bytes accessed | tf_op | source)
XLA Modules:
  0.0 55.9 jit_solution(6856905019652032323)
XLA Ops:
  0.0 0.0 copy-start
  0.0 0.9 %reshape.7 = bf16[4,96]{1,0:T(4,128)(2,1)S(1)} reshape(bf16[2,192]{1,0:T(2,128)(2,1)} %param.11) | data formatting | bytes 1536 | tf_op jit(solution)/shard_map/reshape | solution.py:344
  0.9 0.1 pad.14.prior
  0.9 0.8 %reshape.6 = bf16[4,4000]{1,0:T(4,128)(2,1)S(1)} reshape(bf16[2,2,4000]{2,1,0:T(2,128)(2,1)} %param.9) | data formatting | bytes 64000 | tf_op jit(solution)/shard_map/reshape | solution.py:343
  1.7 1.2 %fusion.3 = (bf16[8,1,4000]{2,1,0:T(2,128)(2,1)S(1)}, bf16[8,1,4000]{2,1,0:T(2,128)(2,1)S(1)}) fusion(bf16[8,2,4000]{2,1,0:T(2,128)(2,1)} %param.16), kind=kLoop, calls=%fused_computation.6 | loop fusion | bytes 256000 | tf_op jit(solution)/shard_map/slice | solution.py:341
  3.0 0.0 copy-start.1
  3.0 0.2 copy_bitcast_fusion
  3.2 0.0 copy-start.3
  3.2 0.0 copy-start.4
  3.2 0.0 copy-start.5
  3.2 0.0 copy-done
  3.2 0.7 %copy-done.1 = f32[9,4000]{1,0:T(8,128)S(1)} copy-done((f32[9,4000]{1,0:T(8,128)S(1)}, f32[9,4000]{1,0:T(8,128)}, u32[]{:S(2)}) %copy-start.1) | copy-done | bytes 144024
  3.9 0.0 copy-done.3
  3.9 0.0 copy-done.4
  4.0 0.0 copy-done.5
  4.0 0.0 copy-start.2
  4.0 0.7 %copy-done.2 = f32[4000]{0:T(1024)S(1)} copy-done((f32[4000]{0:T(1024)S(1)}, f32[4000]{0:T(1024)}, u32[]{:S(2)}) %copy-start.2) | copy-done | bytes 16024
  4.7 50.5 %scores.1 = f32[9,32,256]{2,1,0:T(8,128)S(1)} custom-call(s32[2]{0:T(128)S(1)} %copy-done.3, s32[9]{0:T(128)S(1)} %copy-done.4, s32[8]{0:T(128)S(1)} %copy-done.5, bf16[16,4096]{1,0:T(8,128)(2,1)S(1)} %fusion.2.pc, bf16[4,4096]{1,0:T(4,128)(2,1)S(1)} %pad.13.wp, bf16[4,128]{1,0:T(4,128)(2,1)S(1)} %pad.14.prior, f32[64,4000]{1,0:T(8,128)S(1)} %copy-done, ...), custom_call_target="tpu_custom_call" | custom-call | tf_op jit(solution)/shard_map/scores/pallas_call | solution.py:349
  55.2 0.7 %copy.17 = f32[32,9,256]{2,0,1:T(8,128)} copy(f32[32,9,256]{2,0,1:T(8,128)S(1)} %bitcast.6) | data formatting | bytes 589824
  (2 shorter events, 0.0 us)
Async XLA Ops:
  0.0 3.2 %copy-start = (f32[64,4000]{1,0:T(8,128)S(1)}, f32[64,4000]{1,0:T(8,128)}, u32[]{:S(2)}) copy-start(f32[64,4000]{1,0:T(8,128)} %curves.1) | copy-start | bytes 3072004
  3.0 1.0 %copy-start.1 = (f32[9,4000]{1,0:T(8,128)S(1)}, f32[9,4000]{1,0:T(8,128)}, u32[]{:S(2)}) copy-start(f32[9,4000]{1,0:T(8,128)} %phase.1) | copy-start | bytes 432004
  3.2 0.8 %copy-start.3 = (s32[2]{0:T(128)S(1)}, s32[2]{0:T(128)}, u32[]{:S(2)}) copy-start(s32[2]{0:T(128)} %cls.1) | copy-start | bytes 28
  3.2 0.8 %copy-start.4 = (s32[9]{0:T(128)S(1)}, s32[9]{0:T(128)}, u32[]{:S(2)}) copy-start(s32[9]{0:T(128)} %tri.1) | copy-start | bytes 112
  3.2 0.8 %copy-start.5 = (s32[8]{0:T(128)S(1)}, s32[8]{0:T(128)}, u32[]{:S(2)}) copy-start(s32[8]{0:T(128)} %sub.1) | copy-start | bytes 100
  4.0 0.7 %copy-start.2 = (f32[4000]{0:T(1024)S(1)}, f32[4000]{0:T(1024)}, u32[]{:S(2)}) copy-start(f32[4000]{0:T(1024)} %param.13) | copy-start | bytes 48004

commit v3 on v2

--- a/solution.py
+++ b/solution.py
@@ -21,6 +21,8 @@
 NJ = NY * PJ
 EARLY, LATE = (7, 0, 1), (2, 3, 4, 5, 6)
 GROUPS = ((EARLY, 0, 2), (LATE, 2, 3))
+SPANS = ((0, 0, 8, 0), (0, 8, 8, 0), (1, 0, 8, 16), (1, 8, 9, 16))
+CHUNKS = ((0, 256), (2, 256), (4, 64))
 ROWS = NZ * NX * 8
 
 
@@ -60,7 +62,6 @@
     f32, bf16 = jnp.float32, jnp.bfloat16
     k = curves.shape[1]
     first_rows = lax.broadcasted_iota(jnp.int32, (4, 1), 0) < 2
-    nothing = jnp.zeros((1, (MAIN + 1) * LANES - k), f32)
 
     def curve_row(p):
         total = jnp.zeros((8, k), f32)
@@ -68,21 +69,20 @@
             chosen = lax.broadcasted_iota(jnp.int32, (8, 1), 0) + 8 * g == cls[p]
             total = jnp.where(chosen, curves[pl.ds(8 * g, 8), :], total)
         row = jnp.sum(total, axis=0, keepdims=True)
-        return jnp.concatenate([row * weight[...], nothing], axis=1)
-
-    scaled = wp[...].astype(f32) * jnp.where(first_rows, curve_row(0), curve_row(1))
+        return row * weight[...]
+
+    rows4 = jnp.concatenate([wp[0].astype(f32), wp[1].astype(f32)], axis=0)
+    scaled = rows4 * jnp.where(first_rows, curve_row(0), curve_row(1))
+    prior_f = prior[...].astype(f32)
+    half = prior.shape[1] // 2
+    prior4 = jnp.concatenate(
+        [prior_f[p : p + 1, h * half : (h + 1) * half] for p in (0, 1) for h in (0, 1)], axis=0
+    )
     lane4 = lax.broadcasted_iota(jnp.int32, (4, LANES), 1)
     part4 = lax.broadcasted_iota(jnp.int32, (4, LANES), 0) % 2
     own_class = jnp.where(first_rows, cls[0], cls[1])
     hit = (lane4 == own_class) | ((lane4 == own_class + 64) & (part4 == 0))
-    wide = jnp.concatenate(
-        [
-            scaled[:, : MAIN * LANES],
-            scaled[:, MAIN * LANES :] + prior[...].astype(f32),
-            jnp.where(hit, 1.0, 0.0),
-        ],
-        axis=1,
-    ).astype(bf16)
+    wide = jnp.concatenate([scaled, prior4, jnp.where(hit, 1.0, 0.0)], axis=1).astype(bf16)
     wloc[0] = wide[:, :KH]
     wloc[1] = wide[:, KE - KH :]
     pl.semaphore_wait(barrier, len(peers))
@@ -264,44 +264,51 @@
 
     dims = (((1,), (1,)), ((), ()))
 
-    def cross(part, acc, blocks):
+    def cross(part, acc, blocks, lo, count):
         fresh = True
-        for kh, first, tiles, base in ((0, 0, 8, 0), (0, 8, 8, 0), (1, 0, 8, 16), (1, 8, 9, 16)):
+        for kh, first, tiles, base in SPANS:
             at = pl.ds(first * LANES, tiles * LANES)
             w = [
                 wbuf[kh, rem(zh + d, NZH), :, :, :, at].reshape(ROWS // NZH, tiles * LANES)
                 for d in blocks
             ]
             w = jnp.concatenate(w, axis=0) if len(w) > 1 else w[0]
-            sh = sbuf[part, :, pl.ds((base + first) * LANES, tiles * LANES)]
+            sh = sbuf[part, pl.ds(lo * LANES, count), pl.ds((base + first) * LANES, tiles * LANES)]
             prod = lax.dot_general(w, sh, dims, preferred_element_type=f32)
-            fill = jnp.zeros((prod.shape[0], NS * LANES - NT * NJ), f32)
-            prod = jnp.concatenate([prod, fill], axis=1)
-            for m in range(NS):
+            if count % LANES:
+                fill = jnp.zeros((prod.shape[0], LANES - count % LANES), f32)
+                prod = jnp.concatenate([prod, fill], axis=1)
+            for m in range(prod.shape[1] // LANES):
                 for n, d in enumerate(blocks):
                     slab = prod[n * 64 : (n + 1) * 64, m * LANES : (m + 1) * LANES]
                     rows = pl.ds(d * 64, 64)
-                    acc[m, rows, :] = slab if fresh else acc[m, rows, :] + slab
+                    acc[lo + m, rows, :] = slab if fresh else acc[lo + m, rows, :] + slab
             fresh = False
 
     def finish(blocks):
-        cross(0, acc0, blocks)
-        cross(1, acc1, blocks)
-        for d in blocks:
-            for m in range(NS):
-                val = (
-                    acc0[m, pl.ds(d * 64, 32, stride=2), :]
-                    + acc1[m, pl.ds(d * 64 + 1, 32, stride=2), :]
-                )
-                if d == 0:
-                    rbuf[zh, m] = val
-                else:
-                    ebuf[d - 1, m] = val
-            if d:
-                send(ebuf.at[d - 1], rbuf.at[zh], esend.at[d - 1], erecv.at[d - 1], ep[d - 1])
-
+        for i, (lo, count) in enumerate(CHUNKS):
+            cross(0, acc0, blocks, lo, count)
+            cross(1, acc1, blocks, lo, count)
+            slabs = (count + LANES - 1) // LANES
+            for d in blocks:
+                for m in range(lo, lo + slabs):
+                    val = (
+                        acc0[m, pl.ds(d * 64, 32, stride=2), :]
+                        + acc1[m, pl.ds(d * 64 + 1, 32, stride=2), :]
+                    )
+                    if d == 0:
+                        rbuf[zh, m] = val
+                    else:
+                        ebuf[d - 1, m] = val
+                if d:
+                    at = pl.ds(lo, slabs)
+                    send(
+                        ebuf.at[d - 1, at], rbuf.at[zh, at],
+                        esend.at[d - 1, i], erecv.at[d - 1, i], ep[d - 1],
+                    )
+
+    z_step(4)
     finish((1, 3, 0))
-    z_step(4)
     for g in range(NX):
         arrive(unit_a(1 - core, z_origin(4, 0), g), hsend.at[g], hrecv.at[g], partner)
     finish((2,))
@@ -316,7 +323,9 @@
             yield pltpu.roll(jnp.where(left, swapped, val), PJ * y, 1)
 
     for d in (1, 3, 2):
-        arrive(rbuf.at[rem(zh + NZH - d, NZH)], esend.at[d - 1], erecv.at[d - 1], ep[d - 1])
+        for i, (lo, count) in enumerate(CHUNKS):
+            block = rbuf.at[rem(zh + NZH - d, NZH), pl.ds(lo, (count + LANES - 1) // LANES)]
+            arrive(block, esend.at[d - 1, i], erecv.at[d - 1, i], ep[d - 1])
     for m in range(0, NZH, 2):
         for t, low, high in zip(range(NT), turned(m), turned(m + 1)):
             out[t, :, pl.ds(m * NJ, LANES)] = jnp.where(left, low, high)
@@ -340,8 +349,6 @@
     fill = (MAIN + 1) * LANES - k
     pc = jnp.concatenate([projections[:, 0, :], projections[:, 1, :]], axis=0)
     pc = jnp.pad(pc, ((0, 0), (0, fill)))
-    wp = jnp.pad(particles.reshape(4, k), ((0, 0), (0, fill)))
-    prior = jnp.pad(orient_prior.reshape(4, fill), ((0, 0), (LANES - fill, 0)))
 
     dma = pltpu.SemaphoreType.DMA
     vm = pl.BlockSpec(memory_space=pltpu.VMEM)
@@ -376,8 +383,8 @@
             dma((NX,)),
             dma,
             dma,
-            dma((3,)),
-            dma((3,)),
+            dma((3, len(CHUNKS))),
+            dma((3, len(CHUNKS))),
         ],
         compiler_params=pltpu.CompilerParams(
             collective_id=0, has_side_effects=True, vmem_limit_bytes=48 << 20
@@ -385,7 +392,7 @@
         name="scores",
     )(
         ctf_class, trans_index, orient_subset,
-        pc, wp, prior, ctf_curves, noise_weight[None, :], shift_phase,
+        pc, particles, orient_prior, ctf_curves, noise_weight[None, :], shift_phase,
     )
     return jnp.transpose(scores, (1, 0, 2))
 

time: 56.2 us -> 53.8 us (0.957)
  the two profiles are of different devices: /device:TPU:25 before, /device:TPU:24 now
where the time goes in v3:
time: 53.8 us; the launch traced here: 53.6 us
  Pallas kernels  49.6 us (92%)
  local copies, waits for them, and re-layouts  3.83 us (7%)
    pallas_call x1, Pallas kernels, per_device(): pl.pallas_call(kernel, out_shape=jax.ShapeDtypeStruct((NT, 32, NZH * NJ),...  49.6 us
    unnamed x17, local copies, waits for them, and re-layouts  2.36 us
    slice x1, local copies, waits for them, and re-layouts, per_device(): pc = jnp.concatenate([projections[:, 0, :], projections[:, 1, :]], axis=0)  1.32 us

profile of v3, /device:TPU:24, one launch (start us, length us, event | category | flops | bytes accessed | tf_op | source)
XLA Modules:
  0.0 53.6 jit_solution(10389285442321098496)
XLA Ops:
  0.0 0.0 copy-start
  0.0 1.3 %fusion.3 = (bf16[8,1,4000]{2,1,0:T(2,128)(2,1)S(1)}, bf16[8,1,4000]{2,1,0:T(2,128)(2,1)S(1)}) fusion(bf16[8,2,4000]{2,1,0:T(2,128)(2,1)} %param.16), kind=kLoop, calls=%fused_computation.6 | loop fusion | bytes 256000 | tf_op jit(solution)/shard_map/slice | solution.py:350
  1.3 0.2 copy_bitcast_fusion
  1.5 0.0 copy-start.2
  1.5 0.0 copy-start.3
  1.5 0.0 copy-start.4
  1.5 0.0 copy-start.5
  1.5 0.0 copy-start.6
  1.5 0.0 copy-start.7
  1.6 0.0 copy-done
  1.6 0.7 %copy-done.2 = bf16[2,2,4000]{2,1,0:T(2,128)(2,1)S(1)} copy-done((bf16[2,2,4000]{2,1,0:T(2,128)(2,1)S(1)}, bf16[2,2,4000]{2,1,0:T(2,128)(2,1)}, u32[]{:S(2)}) %copy-start.2) | copy-done | bytes 32024
  2.2 0.0 copy-done.3
  2.3 0.0 copy-done.4
  2.3 0.0 copy-done.5
  2.3 0.0 copy-done.6
  2.3 0.0 copy-done.7
  2.3 0.0 copy-start.1
  2.3 0.9 %copy-done.1 = f32[9,4000]{1,0:T(8,128)S(1)} copy-done((f32[9,4000]{1,0:T(8,128)S(1)}, f32[9,4000]{1,0:T(8,128)}, u32[]{:S(2)}) %copy-start.1) | copy-done | bytes 144024
  3.2 49.6 %scores.1 = f32[9,32,256]{2,1,0:T(8,128)S(1)} custom-call(s32[2]{0:T(128)S(1)} %copy-done.5, s32[9]{0:T(128)S(1)} %copy-done.6, s32[8]{0:T(128)S(1)} %copy-done.7, bf16[16,4096]{1,0:T(8,128)(2,1)S(1)} %fusion.2.pc, bf16[2,2,4000]{2,1,0:T(2,128)(2,1)S(1)} %copy-done.2, bf16[2,192]{1,0:T(2,128)(2,1)S(1)} %copy-done.4, f32[64,4000]{1,0:T(8,128)S(1)} %copy-done, ...), custom_call_target="tpu_custom_call" | custom-call | tf_op jit(solution)/shard_map/scores/pallas_call | solution.py:356
  52.8 0.7 %copy.17 = f32[32,9,256]{2,0,1:T(8,128)} copy(f32[32,9,256]{2,0,1:T(8,128)S(1)} %bitcast.6) | data formatting | bytes 589824
  (1 shorter events, 0.0 us)
Async XLA Ops:
  0.0 1.6 %copy-start = (f32[64,4000]{1,0:T(8,128)S(1)}, f32[64,4000]{1,0:T(8,128)}, u32[]{:S(2)}) copy-start(f32[64,4000]{1,0:T(8,128)} %curves.1) | copy-start | bytes 3072004
  1.5 0.8 %copy-start.2 = (bf16[2,2,4000]{2,1,0:T(2,128)(2,1)S(1)}, bf16[2,2,4000]{2,1,0:T(2,128)(2,1)}, u32[]{:S(2)}) copy-start(bf16[2,2,4000]{2,1,0:T(2,128)(2,1)} %wp.1) | copy-start | bytes 96004
  1.5 0.8 %copy-start.3 = (f32[4000]{0:T(1024)S(1)}, f32[4000]{0:T(1024)}, u32[]{:S(2)}) copy-start(f32[4000]{0:T(1024)} %param.13) | copy-start | bytes 48004
  1.5 0.7 %copy-start.4 = (bf16[2,192]{1,0:T(2,128)(2,1)S(1)}, bf16[2,192]{1,0:T(2,128)(2,1)}, u32[]{:S(2)}) copy-start(bf16[2,192]{1,0:T(2,128)(2,1)} %prior.1) | copy-start | bytes 2308
  1.5 0.7 %copy-start.5 = (s32[2]{0:T(128)S(1)}, s32[2]{0:T(128)}, u32[]{:S(2)}) copy-start(s32[2]{0:T(128)} %cls.1) | copy-start | bytes 28
  1.5 0.7 %copy-start.6 = (s32[9]{0:T(128)S(1)}, s32[9]{0:T(128)}, u32[]{:S(2)}) copy-start(s32[9]{0:T(128)} %tri.1) | copy-start | bytes 112
  1.5 0.7 %copy-start.7 = (s32[8]{0:T(128)S(1)}, s32[8]{0:T(128)}, u32[]{:S(2)}) copy-start(s32[8]{0:T(128)} %sub.1) | copy-start | bytes 100
  2.3 1.0 %copy-start.1 = (f32[9,4000]{1,0:T(8,128)S(1)}, f32[9,4000]{1,0:T(8,128)}, u32[]{:S(2)}) copy-start(f32[9,4000]{1,0:T(8,128)} %phase.1) | copy-start | bytes 432004

commit v4 on v3

--- a/solution.py
+++ b/solution.py
@@ -251,11 +251,11 @@
     shift(0)
     y_step(2)
     z_step(2)
+    y_step(3)
     shift(6)
-    y_step(3)
     z_step(3)
+    y_step(4)
     shift(2)
-    y_step(4)
     shift(4)
     p_wait(0, 0)
     for s in range(1, 4):

time: 53.8 us -> 54.2 us (level)
  no operation moved by 1% of the time
where the time goes in v4:
time: 54.2 us; the launch traced here: 54 us
  Pallas kernels  50 us (92%)
  local copies, waits for them, and re-layouts  3.83 us (7%)
    pallas_call x1, Pallas kernels, per_device(): pl.pallas_call(kernel, out_shape=jax.ShapeDtypeStruct((NT, 32, NZH * NJ),...  50 us
    unnamed x17, local copies, waits for them, and re-layouts  2.36 us
    slice x1, local copies, waits for them, and re-layouts, per_device(): pc = jnp.concatenate([projections[:, 0, :], projections[:, 1, :]], axis=0)  1.32 us

profile of v4, /device:TPU:24, one launch (start us, length us, event | category | flops | bytes accessed | tf_op | source)
XLA Modules:
  0.0 54.0 jit_solution(7258528450100751254)
XLA Ops:
  0.0 0.0 copy-start
  0.0 1.3 %fusion.3 = (bf16[8,1,4000]{2,1,0:T(2,128)(2,1)S(1)}, bf16[8,1,4000]{2,1,0:T(2,128)(2,1)S(1)}) fusion(bf16[8,2,4000]{2,1,0:T(2,128)(2,1)} %param.16), kind=kLoop, calls=%fused_computation.6 | loop fusion | bytes 256000 | tf_op jit(solution)/shard_map/slice | solution.py:350
  1.3 0.2 copy_bitcast_fusion
  1.5 0.0 copy-start.2
  1.5 0.0 copy-start.3
  1.5 0.0 copy-start.4
  1.5 0.0 copy-start.5
  1.5 0.0 copy-start.6
  1.5 0.0 copy-start.7
  1.6 0.0 copy-done
  1.6 0.7 %copy-done.2 = bf16[2,2,4000]{2,1,0:T(2,128)(2,1)S(1)} copy-done((bf16[2,2,4000]{2,1,0:T(2,128)(2,1)S(1)}, bf16[2,2,4000]{2,1,0:T(2,128)(2,1)}, u32[]{:S(2)}) %copy-start.2) | copy-done | bytes 32024
  2.2 0.0 copy-done.3
  2.3 0.0 copy-done.4
  2.3 0.0 copy-done.5
  2.3 0.0 copy-done.6
  2.3 0.0 copy-done.7
  2.3 0.0 copy-start.1
  2.3 0.9 %copy-done.1 = f32[9,4000]{1,0:T(8,128)S(1)} copy-done((f32[9,4000]{1,0:T(8,128)S(1)}, f32[9,4000]{1,0:T(8,128)}, u32[]{:S(2)}) %copy-start.1) | copy-done | bytes 144024
  3.2 50.0 %scores.1 = f32[9,32,256]{2,1,0:T(8,128)S(1)} custom-call(s32[2]{0:T(128)S(1)} %copy-done.5, s32[9]{0:T(128)S(1)} %copy-done.6, s32[8]{0:T(128)S(1)} %copy-done.7, bf16[16,4096]{1,0:T(8,128)(2,1)S(1)} %fusion.2.pc, bf16[2,2,4000]{2,1,0:T(2,128)(2,1)S(1)} %copy-done.2, bf16[2,192]{1,0:T(2,128)(2,1)S(1)} %copy-done.4, f32[64,4000]{1,0:T(8,128)S(1)} %copy-done, ...), custom_call_target="tpu_custom_call" | custom-call | tf_op jit(solution)/shard_map/scores/pallas_call | solution.py:356
  53.2 0.7 %copy.17 = f32[32,9,256]{2,0,1:T(8,128)} copy(f32[32,9,256]{2,0,1:T(8,128)S(1)} %bitcast.6) | data formatting | bytes 589824
  (1 shorter events, 0.0 us)
Async XLA Ops:
  0.0 1.6 %copy-start = (f32[64,4000]{1,0:T(8,128)S(1)}, f32[64,4000]{1,0:T(8,128)}, u32[]{:S(2)}) copy-start(f32[64,4000]{1,0:T(8,128)} %curves.1) | copy-start | bytes 3072004
  1.5 0.8 %copy-start.2 = (bf16[2,2,4000]{2,1,0:T(2,128)(2,1)S(1)}, bf16[2,2,4000]{2,1,0:T(2,128)(2,1)}, u32[]{:S(2)}) copy-start(bf16[2,2,4000]{2,1,0:T(2,128)(2,1)} %wp.1) | copy-start | bytes 96004
  1.5 0.8 %copy-start.3 = (f32[4000]{0:T(1024)S(1)}, f32[4000]{0:T(1024)}, u32[]{:S(2)}) copy-start(f32[4000]{0:T(1024)} %param.13) | copy-start | bytes 48004
  1.5 0.7 %copy-start.4 = (bf16[2,192]{1,0:T(2,128)(2,1)S(1)}, bf16[2,192]{1,0:T(2,128)(2,1)}, u32[]{:S(2)}) copy-start(bf16[2,192]{1,0:T(2,128)(2,1)} %prior.1) | copy-start | bytes 2308
  1.5 0.7 %copy-start.5 = (s32[2]{0:T(128)S(1)}, s32[2]{0:T(128)}, u32[]{:S(2)}) copy-start(s32[2]{0:T(128)} %cls.1) | copy-start | bytes 28
  1.5 0.7 %copy-start.6 = (s32[9]{0:T(128)S(1)}, s32[9]{0:T(128)}, u32[]{:S(2)}) copy-start(s32[9]{0:T(128)} %tri.1) | copy-start | bytes 112
  1.5 0.7 %copy-start.7 = (s32[8]{0:T(128)S(1)}, s32[8]{0:T(128)}, u32[]{:S(2)}) copy-start(s32[8]{0:T(128)} %sub.1) | copy-start | bytes 100
  2.3 1.0 %copy-start.1 = (f32[9,4000]{1,0:T(8,128)S(1)}, f32[9,4000]{1,0:T(8,128)}, u32[]{:S(2)}) copy-start(f32[9,4000]{1,0:T(8,128)} %phase.1) | copy-start | bytes 432004
